TPU v7x, 512 devices: a whole 4x8x8 slice. The times are simulated.
512 devices in a mesh: seq: 64 (over y_lo, z, core), ch: 8 (over y_hi, x).
Axes of the slice: x: 4, y: 8 (y_hi: 2, y_lo: 4; y = y_hi * 4 + y_lo), z: 8, core: 2. Of those that a mesh axis runs over, the one named last changes fastest.
Arguments:
- grad_out: bfloat16 [16384, 4096], P('seq', 'ch'), may hold values from -6 to 6
- saved_in: bfloat16 [16384, 4096], P('seq', 'ch'), may hold values from -6 to 6
- filter_taps: bfloat16 [256, 4096], P(None, 'ch'), may hold values from -0.375 to 0.375
- skip_gain: float32 [4096], P('ch'), may hold values from 0.5 to 1.5
- projection: bfloat16 [4096, 4096], P('seq', 'ch'), may hold values from -0.09375 to 0.09375
Outputs:
- grad_in: bfloat16 [16384, 4096], P('seq', 'ch')
- filter_grad: float32 [256, 4096], P('seq', 'ch')
All inputs are finite; a program needn't handle non-finite values.
Results may differ from a plain program's by a relative error of at most 0.015.
Values may be sent and summed in bfloat16 or wider, within the bound.
A program may use at most 64 MiB of HBM per device.

v0:
```python
import math

import jax
import jax.numpy as jnp
from jax import lax
from jax.sharding import PartitionSpec as P


def passed_along(value, axis, steps):
    count = lax.axis_size(axis)
    leading, last = (max(0, -steps), min(count, count - steps))
    return lax.ppermute(value, axis, [(source, source + steps) for source in range(leading, last)])


def swapped(x, axis, stride):
    return lax.ppermute(x, axis, [(i, i ^ 1 << stride) for i in range(lax.axis_size(axis))])


def window(signal, kernel):
    result = lax.conv_general_dilated(
        signal[None],
        kernel[:, None, :],
        (1,),
        [(0, 0)],
        dimension_numbers=("NWC", "WIO", "NWC"),
        feature_group_count=signal.shape[1],
        preferred_element_type=jnp.float32,
    )
    return result[0]


def neighbours(upper_pair, lower_pair):
    from_above = passed_along(upper_pair, "seq", -1)
    from_below = passed_along(lower_pair, "seq", 1)
    return (from_above, from_below)


def mirror_inputs(stacked):
    bit_count = lax.axis_size(("seq", "ch")).bit_length() - 1
    for bit_index in range(bit_count):
        stacked = swapped(stacked, ("seq", "ch"), bit_index)
    return stacked


def mirror_result(values):
    bit_count = lax.axis_size(("seq", "ch")).bit_length() - 1
    for bit_index in range(bit_count):
        values = swapped(values, ("seq", "ch"), bit_index)
    return values


def seq_total(partials):
    return (lax.psum_scatter(partials[0], "seq", scatter_dimension=0, tiled=True),)


def body(grad_out, saved_in, filter_taps, skip_gain, projection):
    tok_rows = grad_out.shape[0]
    edge = 2 * tok_rows - 1
    mirrored = mirror_inputs(jnp.stack([grad_out, saved_in]))
    rc_grad = mirrored[0, ::-1, ::-1]
    rc_input = mirrored[1, ::-1, ::-1]
    upper_rows, lower_rows = neighbours(
        jnp.stack([grad_out, rc_grad]), jnp.stack([saved_in, rc_input])
    )
    conv_forward = window(jnp.concatenate([grad_out, upper_rows[0]], axis=0)[:edge], filter_taps)
    conv_mirror = window(jnp.concatenate([rc_grad, upper_rows[1]], axis=0)[:edge], filter_taps)
    taps_forward = window(jnp.concatenate([lower_rows[0], saved_in], axis=0)[1:], grad_out)[::-1]
    taps_mirror = window(jnp.concatenate([lower_rows[1], rc_input], axis=0)[1:], rc_grad)[::-1]
    returned = mirror_result(conv_mirror[::-1, ::-1])
    conv_sum = conv_forward + returned
    filter_part = seq_total((taps_forward + taps_mirror,))[0]
    grad_conv = (conv_sum + skip_gain[None, :] * grad_out.astype(jnp.float32)).astype(jnp.bfloat16)
    partial_value = lax.dot_general(
        grad_conv,
        lax.all_gather(projection, "seq", axis=0, tiled=True),
        (((1,), (1,)), ((), ())),
        preferred_element_type=jnp.float32,
    )
    grad_in = lax.psum_scatter(
        partial_value.astype(jnp.bfloat16), "ch", scatter_dimension=1, tiled=True
    )
    total_rows = tok_rows * lax.axis_size("seq")
    filter_grad = filter_part * (1.0 / math.sqrt(total_rows))
    return (grad_in, filter_grad)


def solution(mesh):
    placed = (P("seq", "ch"), P("seq", "ch"), P(None, "ch"), P("ch"), P("seq", "ch"))
    return jax.shard_map(
        body,
        mesh=mesh,
        in_specs=placed,
        out_specs=(P("seq", "ch"), P("seq", "ch")),
        check_vma=False,
    )
```

profile of v0, /device:TPU:1, one launch (start us, length us, event | category | flops | bytes accessed | tf_op | source)
XLA Modules:
  0.0 1019.4 jit_solution(17271620590732437729)
XLA Ops:
  18.9 9.6 collective-permute-start.1
  28.5 9.6 collective-permute-done.1
  38.2 8.4 collective-permute-start.2
  46.6 13.3 %collective-permute-done.2 = bf16[2,256,512]{2,1,0:T(8,128)(2,1)S(1)} collective-permute-done((bf16[2,256,512]{2,1,0:T(8,128)(2,1)S(1)}, bf16[2,256,512]{2,1,0:T(8,128)(2,1)S(1)}, u32[]{:S(2)}, u32[]{:S(2)}) %collective-permute-start.2) | collective-permute-done | bytes 524320 | tf_op jit(solution)/shard_map/ppermute | solution.py:16
  59.8 12.0 %collective-permute-start.3 = (bf16[2,256,512]{2,1,0:T(8,128)(2,1)S(1)}, bf16[2,256,512]{2,1,0:T(8,128)(2,1)S(1)}, u32[]{:S(2)}, u32[]{:S(2)}) collective-permute-start(bf16[2,256,512]{2,1,0:T(8,128)(2,1)S(1)} %collective-permute-done.2), channel_id=1, source_target_pairs={{0,8},{1,9},{2,10},{3,11},{4,12},{5,13},{6,14},{7,15},{8,0},{9,1},... | collective-permute-start | bytes 1572872 | tf_op jit(solution)/shard_map/ppermute | solution.py:16
  77.4 12.0 %collective-permute-done.4 = bf16[2,256,512]{2,1,0:T(8,128)(2,1)S(1)} collective-permute-done((bf16[2,256,512]{2,1,0:T(8,128)(2,1)S(1)}, bf16[2,256,512]{2,1,0:T(8,128)(2,1)S(1)}, u32[]{:S(2)}, u32[]{:S(2)}) %collective-permute-start.4) | collective-permute-done | bytes 524320 | tf_op jit(solution)/shard_map/ppermute | solution.py:16
  95.2 22.7 %collective-permute-done.5 = bf16[2,256,512]{2,1,0:T(8,128)(2,1)S(1)} collective-permute-done((bf16[2,256,512]{2,1,0:T(8,128)(2,1)S(1)}, bf16[2,256,512]{2,1,0:T(8,128)(2,1)S(1)}, u32[]{:S(2)}, u32[]{:S(2)}) %collective-permute-start.5) | collective-permute-done | bytes 524320 | tf_op jit(solution)/shard_map/ppermute | solution.py:16
  125.9 22.1 %collective-permute-done.6 = bf16[2,256,512]{2,1,0:T(8,128)(2,1)S(1)} collective-permute-done((bf16[2,256,512]{2,1,0:T(8,128)(2,1)S(1)}, bf16[2,256,512]{2,1,0:T(8,128)(2,1)S(1)}, u32[]{:S(2)}, u32[]{:S(2)}) %collective-permute-start.6) | collective-permute-done | bytes 524320 | tf_op jit(solution)/shard_map/ppermute | solution.py:16
  150.9 10.3 %collective-permute-done.7 = bf16[2,256,512]{2,1,0:T(8,128)(2,1)S(1)} collective-permute-done((bf16[2,256,512]{2,1,0:T(8,128)(2,1)S(1)}, bf16[2,256,512]{2,1,0:T(8,128)(2,1)S(1)}, u32[]{:S(2)}, u32[]{:S(2)}) %collective-permute-start.7) | collective-permute-done | bytes 524320 | tf_op jit(solution)/shard_map/ppermute | solution.py:16
  166.0 23.5 %collective-permute-done.8 = bf16[2,256,512]{2,1,0:T(8,128)(2,1)S(1)} collective-permute-done((bf16[2,256,512]{2,1,0:T(8,128)(2,1)S(1)}, bf16[2,256,512]{2,1,0:T(8,128)(2,1)S(1)}, u32[]{:S(2)}, u32[]{:S(2)}) %collective-permute-start.8) | collective-permute-done | bytes 524320 | tf_op jit(solution)/shard_map/ppermute | solution.py:16
  202.1 13.5 %fusion.4 = f32[1,256,512]{2,0,1:T(1,128)S(1)} fusion(bf16[1,511,512]{2,1,0:T(8,128)(2,1)S(1)} %fusion.10, bf16[256,1,512]{2,0,1:T(8,128)(2,1)S(1)} %bitcast.42), kind=kOutput, calls=%fused_computation.5 | convolution fusion | flops 67108864 | bytes 1309696 | tf_op jit(solution)/shard_map/conv_general_dilated | solution.py:20
  230.9 8.8 collective-permute-done.11
  247.2 19.4 %collective-permute-done.12 = f32[256,512]{1,0:T(8,128)S(1)} collective-permute-done((f32[256,512]{1,0:T(8,128)S(1)}, f32[256,512]{1,0:T(8,128)S(1)}, u32[]{:S(2)}, u32[]{:S(2)}) %collective-permute-start.12) | collective-permute-done | bytes 524320 | tf_op jit(solution)/shard_map/ppermute | solution.py:16
  278.0 10.8 %collective-permute-done.14 = f32[256,512]{1,0:T(8,128)S(1)} collective-permute-done((f32[256,512]{1,0:T(8,128)S(1)}, f32[256,512]{1,0:T(8,128)S(1)}, u32[]{:S(2)}, u32[]{:S(2)}) %collective-permute-start.14) | collective-permute-done | bytes 524320 | tf_op jit(solution)/shard_map/ppermute | solution.py:16
  288.8 16.6 %collective-permute-start.15 = (f32[256,512]{1,0:T(8,128)S(1)}, f32[256,512]{1,0:T(8,128)S(1)}, u32[]{:S(2)}, u32[]{:S(2)}) collective-permute-start(f32[256,512]{1,0:T(8,128)S(1)} %collective-permute-done.14), channel_id=1, source_target_pairs={{0,32},{1,33},{2,34},{3,35},{4,36},{5,37},{6,38},{7,39},{8,40},{9,... | collective-permute-start | bytes 1572872 | tf_op jit(solution)/shard_map/ppermute | solution.py:16
  305.7 23.5 %collective-permute-done.15 = f32[256,512]{1,0:T(8,128)S(1)} collective-permute-done((f32[256,512]{1,0:T(8,128)S(1)}, f32[256,512]{1,0:T(8,128)S(1)}, u32[]{:S(2)}, u32[]{:S(2)}) %collective-permute-start.15) | collective-permute-done | bytes 524320 | tf_op jit(solution)/shard_map/ppermute | solution.py:16
  329.2 9.5 collective-permute-start.16
  338.7 13.5 %fusion = f32[1,256,512]{2,0,1:T(1,128)S(1)} fusion(bf16[1,511,512]{2,1,0:T(8,128)(2,1)S(1)} %get-tuple-element.8, bf16[256,1,512]{2,0,1:T(8,128)(2,1)S(1)} %bitcast.47), kind=kOutput, calls=%fused_computation.1 | convolution fusion | flops 67108864 | bytes 1309696 | tf_op jit(solution)/shard_map/conv_general_dilated | solution.py:20
  352.2 10.1 collective-permute-done.16
  364.4 13.5 %fusion.2 = f32[1,256,512]{2,0,1:T(1,128)S(1)} fusion(bf16[1,511,512]{2,1,0:T(8,128)(2,1)S(1)} %get-tuple-element.9, bf16[256,1,512]{2,0,1:T(8,128)(2,1)S(1)} %bitcast.45), kind=kOutput, calls=%fused_computation.3 | convolution fusion | flops 67108864 | bytes 1309696 | tf_op jit(solution)/shard_map/conv_general_dilated | solution.py:20
  383.1 13.5 %fusion.6 = f32[1,256,512]{2,0,1:T(1,128)S(1)} fusion(bf16[1,511,512]{2,1,0:T(8,128)(2,1)S(1)} %fusion.11, bf16[256,1,512]{2,0,1:T(8,128)(2,1)S(1)} %bitcast.41), kind=kOutput, calls=%fused_computation.7 | convolution fusion | flops 67108864 | bytes 1309696 | tf_op jit(solution)/shard_map/conv_general_dilated | solution.py:20
  396.6 9.8 collective-permute-done.18
  413.2 500.1 %all-reduce.3.cloned.1.call-done = f32[256,512]{1,0:T(8,128)} async-done(((f32[256,512]{1,0:T(8,128)}), f32[256,512]{1,0:T(8,128)}) %all-reduce.3.cloned.1.call-update) | async-done | bytes 524304
  914.6 98.2 %reduce-scatter.2.cloned.1.call-done = bf16[256,512]{1,0:T(8,128)(2,1)} async-done(((bf16[256,4096]{1,0:T(8,128)(2,1)}), bf16[256,512]{1,0:T(8,128)(2,1)}) %reduce-scatter.2.cloned.1.call-update) | async-done | bytes 262160 | tf_op jit(solution)/shard_map/reduce_scatter | solution.py:79
  (58 shorter events, 100.4 us)
Async XLA Ops:
  7.2 194.9 %copy-start = (bf16[256,512]{1,0:T(8,128)(2,1)S(1)}, bf16[256,512]{1,0:T(8,128)(2,1)}, u32[]{:S(2)}) copy-start(bf16[256,512]{1,0:T(8,128)(2,1)} %param.7) | copy-start | bytes 786436
  7.2 389.4 %all-gather.2.cloned.1.call-start = ((), (), s32[]{:S(2)}) async-start(), calls=%async_computation.1 | async-start | bytes 4259840 | tf_op jit(solution)/shard_map/all_gather | solution.py:75
  8.3 10.6 %collective-permute-start = (bf16[2,256,512]{2,1,0:T(8,128)(2,1)S(1)}, bf16[2,256,512]{2,1,0:T(8,128)(2,1)S(1)}, u32[]{:S(2)}, u32[]{:S(2)}) collective-permute-start(bf16[2,256,512]{2,1,0:T(8,128)(2,1)S(1)} %pad_maximum_fusion), channel_id=1, source_target_pairs={{0,1},{1,0},{2,3},{3,2},{4,5},{5,4},{6,7},{7,6},{8,9},{9,8},{10,11... | collective-permute-start | bytes 1572872 | tf_op jit(solution)/shard_map/ppermute | solution.py:16
  18.9 19.2 %collective-permute-start.1 = (bf16[2,256,512]{2,1,0:T(8,128)(2,1)S(1)}, bf16[2,256,512]{2,1,0:T(8,128)(2,1)S(1)}, u32[]{:S(2)}, u32[]{:S(2)}) collective-permute-start(bf16[2,256,512]{2,1,0:T(8,128)(2,1)S(1)} %collective-permute-done), channel_id=1, source_target_pairs={{0,2},{1,3},{2,0},{3,1},{4,6},{5,7},{6,4},{7,5},{8,10},{9,11},{10,... | collective-permute-start | bytes 1572872 | tf_op jit(solution)/shard_map/ppermute | solution.py:16
  38.2 21.7 %collective-permute-start.2 = (bf16[2,256,512]{2,1,0:T(8,128)(2,1)S(1)}, bf16[2,256,512]{2,1,0:T(8,128)(2,1)S(1)}, u32[]{:S(2)}, u32[]{:S(2)}) collective-permute-start(bf16[2,256,512]{2,1,0:T(8,128)(2,1)S(1)} %collective-permute-done.1), channel_id=1, source_target_pairs={{0,4},{1,5},{2,6},{3,7},{4,0},{5,1},{6,2},{7,3},{8,12},{9,13},{10,... | collective-permute-start | bytes 1572872 | tf_op jit(solution)/shard_map/ppermute | solution.py:16
  59.8 13.6 %collective-permute-start.3 = (bf16[2,256,512]{2,1,0:T(8,128)(2,1)S(1)}, bf16[2,256,512]{2,1,0:T(8,128)(2,1)S(1)}, u32[]{:S(2)}, u32[]{:S(2)}) collective-permute-start(bf16[2,256,512]{2,1,0:T(8,128)(2,1)S(1)} %collective-permute-done.2), channel_id=1, source_target_pairs={{0,8},{1,9},{2,10},{3,11},{4,12},{5,13},{6,14},{7,15},{8,0},{9,1},... | collective-permute-start | bytes 1572872 | tf_op jit(solution)/shard_map/ppermute | solution.py:16
  73.4 16.0 %collective-permute-start.4 = (bf16[2,256,512]{2,1,0:T(8,128)(2,1)S(1)}, bf16[2,256,512]{2,1,0:T(8,128)(2,1)S(1)}, u32[]{:S(2)}, u32[]{:S(2)}) collective-permute-start(bf16[2,256,512]{2,1,0:T(8,128)(2,1)S(1)} %collective-permute-done.3), channel_id=1, source_target_pairs={{0,16},{1,17},{2,18},{3,19},{4,20},{5,21},{6,22},{7,23},{8,24},{9,... | collective-permute-start | bytes 1572872 | tf_op jit(solution)/shard_map/ppermute | solution.py:16
  89.4 28.5 %collective-permute-start.5 = (bf16[2,256,512]{2,1,0:T(8,128)(2,1)S(1)}, bf16[2,256,512]{2,1,0:T(8,128)(2,1)S(1)}, u32[]{:S(2)}, u32[]{:S(2)}) collective-permute-start(bf16[2,256,512]{2,1,0:T(8,128)(2,1)S(1)} %collective-permute-done.4), channel_id=1, source_target_pairs={{0,32},{1,33},{2,34},{3,35},{4,36},{5,37},{6,38},{7,39},{8,40},{9,... | collective-permute-start | bytes 1572872 | tf_op jit(solution)/shard_map/ppermute | solution.py:16
  117.9 30.1 %collective-permute-start.6 = (bf16[2,256,512]{2,1,0:T(8,128)(2,1)S(1)}, bf16[2,256,512]{2,1,0:T(8,128)(2,1)S(1)}, u32[]{:S(2)}, u32[]{:S(2)}) collective-permute-start(bf16[2,256,512]{2,1,0:T(8,128)(2,1)S(1)} %collective-permute-done.5), channel_id=1, source_target_pairs={{0,64},{1,65},{2,66},{3,67},{4,68},{5,69},{6,70},{7,71},{8,72},{9,... | collective-permute-start | bytes 1572872 | tf_op jit(solution)/shard_map/ppermute | solution.py:16
  148.0 13.1 %collective-permute-start.7 = (bf16[2,256,512]{2,1,0:T(8,128)(2,1)S(1)}, bf16[2,256,512]{2,1,0:T(8,128)(2,1)S(1)}, u32[]{:S(2)}, u32[]{:S(2)}) collective-permute-start(bf16[2,256,512]{2,1,0:T(8,128)(2,1)S(1)} %collective-permute-done.6), channel_id=1, source_target_pairs={{0,128},{1,129},{2,130},{3,131},{4,132},{5,133},{6,134},{7,135},{8... | collective-permute-start | bytes 1572872 | tf_op jit(solution)/shard_map/ppermute | solution.py:16
  161.1 28.3 %collective-permute-start.8 = (bf16[2,256,512]{2,1,0:T(8,128)(2,1)S(1)}, bf16[2,256,512]{2,1,0:T(8,128)(2,1)S(1)}, u32[]{:S(2)}, u32[]{:S(2)}) collective-permute-start(bf16[2,256,512]{2,1,0:T(8,128)(2,1)S(1)} %collective-permute-done.7), channel_id=1, source_target_pairs={{0,256},{1,257},{2,258},{3,259},{4,260},{5,261},{6,262},{7,263},{8... | collective-permute-start | bytes 1572872 | tf_op jit(solution)/shard_map/ppermute | solution.py:16
  191.5 10.5 %collective-permute-start.9 = (bf16[2,256,512]{2,1,0:T(8,128)(2,1)S(1)}, bf16[2,256,512]{2,1,0:T(8,128)(2,1)S(1)}, u32[]{:S(2)}, u32[]{:S(2)}) collective-permute-start(bf16[2,256,512]{2,1,0:T(8,128)(2,1)S(1)} %pad_maximum_fusion.1), channel_id=1, source_target_pairs={{8,0},{16,8},{24,16},{32,24},{40,32},{48,40},{56,48},{64,56},{72,6... | collective-permute-start | bytes 1572872 | tf_op jit(solution)/shard_map/ppermute | solution.py:12
  194.0 719.3 %all-reduce.3.cloned.1.call-start = ((), (), s32[]{:S(2)}) async-start(), calls=%async_computation.3 | async-start | bytes 1048576
  216.3 9.9 collective-permute-start.10
  226.3 13.4 %collective-permute-start.11 = (f32[256,512]{1,0:T(8,128)S(1)}, f32[256,512]{1,0:T(8,128)S(1)}, u32[]{:S(2)}, u32[]{:S(2)}) collective-permute-start(f32[256,512]{1,0:T(8,128)S(1)} %collective-permute-done.10), channel_id=1, source_target_pairs={{0,2},{1,3},{2,0},{3,1},{4,6},{5,7},{6,4},{7,5},{8,10},{9,11},{10,... | collective-permute-start | bytes 1572872 | tf_op jit(solution)/shard_map/ppermute | solution.py:16
  239.7 26.9 %collective-permute-start.12 = (f32[256,512]{1,0:T(8,128)S(1)}, f32[256,512]{1,0:T(8,128)S(1)}, u32[]{:S(2)}, u32[]{:S(2)}) collective-permute-start(f32[256,512]{1,0:T(8,128)S(1)} %collective-permute-done.11), channel_id=1, source_target_pairs={{0,4},{1,5},{2,6},{3,7},{4,0},{5,1},{6,2},{7,3},{8,12},{9,13},{10,... | collective-permute-start | bytes 1572872 | tf_op jit(solution)/shard_map/ppermute | solution.py:16
  266.6 3.8 collective-permute-start.13
  270.4 18.4 %collective-permute-start.14 = (f32[256,512]{1,0:T(8,128)S(1)}, f32[256,512]{1,0:T(8,128)S(1)}, u32[]{:S(2)}, u32[]{:S(2)}) collective-permute-start(f32[256,512]{1,0:T(8,128)S(1)} %collective-permute-done.13), channel_id=1, source_target_pairs={{0,16},{1,17},{2,18},{3,19},{4,20},{5,21},{6,22},{7,23},{8,24},{9,... | collective-permute-start | bytes 1572872 | tf_op jit(solution)/shard_map/ppermute | solution.py:16
  275.8 29.6 %collective-permute-start.19 = (bf16[2,256,512]{2,1,0:T(8,128)(2,1)S(1)}, bf16[2,256,512]{2,1,0:T(8,128)(2,1)S(1)}, u32[]{:S(2)}, u32[]{:S(2)}) collective-permute-start(bf16[2,256,512]{2,1,0:T(8,128)(2,1)S(1)} %pad_maximum_fusion.6), channel_id=1, source_target_pairs={{0,8},{8,16},{16,24},{24,32},{32,40},{40,48},{48,56},{56,64},{64,7... | collective-permute-start | bytes 1572872 | tf_op jit(solution)/shard_map/ppermute | solution.py:12
  288.8 40.4 %collective-permute-start.15 = (f32[256,512]{1,0:T(8,128)S(1)}, f32[256,512]{1,0:T(8,128)S(1)}, u32[]{:S(2)}, u32[]{:S(2)}) collective-permute-start(f32[256,512]{1,0:T(8,128)S(1)} %collective-permute-done.14), channel_id=1, source_target_pairs={{0,32},{1,33},{2,34},{3,35},{4,36},{5,37},{6,38},{7,39},{8,40},{9,... | collective-permute-start | bytes 1572872 | tf_op jit(solution)/shard_map/ppermute | solution.py:16
  329.2 33.1 %collective-permute-start.16 = (f32[256,512]{1,0:T(8,128)S(1)}, f32[256,512]{1,0:T(8,128)}, u32[]{:S(2)}, u32[]{:S(2)}) collective-permute-start(f32[256,512]{1,0:T(8,128)S(1)} %collective-permute-done.15), channel_id=1, source_target_pairs={{0,64},{1,65},{2,66},{3,67},{4,68},{5,69},{6,70},{7,71},{8,72},{9,... | collective-permute-start | bytes 1572872 | tf_op jit(solution)/shard_map/ppermute | solution.py:16
  362.3 17.3 %collective-permute-start.17 = (f32[256,512]{1,0:T(8,128)}, f32[256,512]{1,0:T(8,128)S(1)}, u32[]{:S(2)}, u32[]{:S(2)}) collective-permute-start(f32[256,512]{1,0:T(8,128)} %collective-permute-done.16), channel_id=1, source_target_pairs={{0,128},{1,129},{2,130},{3,131},{4,132},{5,133},{6,134},{7,135},{8... | collective-permute-start | bytes 1572872 | tf_op jit(solution)/shard_map/ppermute | solution.py:16
  379.5 633.4 %reduce-scatter.2.cloned.1.call-start = ((), (), s32[]{:S(2)}) async-start(), calls=%async_computation.2 | async-start | bytes 2359296 | tf_op jit(solution)/shard_map/reduce_scatter | solution.py:79
  379.6 26.8 %collective-permute-start.18 = (f32[256,512]{1,0:T(8,128)S(1)}, f32[256,512]{1,0:T(8,128)S(1)}, u32[]{:S(2)}, u32[]{:S(2)}) collective-permute-start(f32[256,512]{1,0:T(8,128)S(1)} %collective-permute-done.17), channel_id=1, source_target_pairs={{0,256},{1,257},{2,258},{3,259},{4,260},{5,261},{6,262},{7,263},{8... | collective-permute-start | bytes 1572872 | tf_op jit(solution)/shard_map/ppermute | solution.py:16
  (3 other events, 126.2 us)
Sparse Core Ops, SparseCore 0:
  194.1 159.8 all-gather.1
  379.6 533.6 all-reduce.2
  919.2 93.5 reduce-scatter.1
where the time goes:
time: 1020 us
  waiting for transfers between devices  819 us (80%)
  starting transfers between devices  117 us (11%)
  matrix products  58.8 us (6%)
  between operations  14.8 us (1%)
    unnamed x4, waiting for transfers between devices  500 us
    ppermute x18, waiting for transfers between devices, swapped(): lax.ppermute(x, axis, [(i, i ^ 1 << stride) for i in range(lax.axis_size(...  213 us
    ppermute x18, starting transfers between devices, swapped(): lax.ppermute(x, axis, [(i, i ^ 1 << stride) for i in range(lax.axis_size(...  113 us
    reduce_scatter x1, waiting for transfers between devices, body(): lax.psum_scatter(partial_value.astype(jnp.bfloat16), 'ch', scatter_dimens...  98.2 us
    conv_general_dilated x4, matrix products, window(): lax.conv_general_dilated(signal[None], kernel[:, None, :], (1,), [(0, 0)]...  53.9 us
  transfers between devices with their start and end apart: 23, of which 20 were waited for; matrix products, arithmetic and copies ran while one was open for 6% of the time, Pallas kernels for 0%

commit v1 on v0

v1 whole, which is shorter than its diff:
```python
import math

import jax
import jax.numpy as jnp
import ml_dtypes
import numpy as np
from jax import lax
from jax.sharding import PartitionSpec as P


def half_bin_basis(rows):
    size = 2 * rows
    angle = 2.0 * np.pi * np.outer(np.arange(rows) + 0.5, np.arange(rows)) / size
    return np.concatenate([np.cos(angle), -np.sin(angle)], axis=0)


def bf16(values):
    return jnp.asarray(values.astype(ml_dtypes.bfloat16))


def split(spectrum):
    half = spectrum.shape[0] // 2
    return spectrum[:half], spectrum[half:]


def body(grad_out, saved_in, filter_taps, skip_gain, projection):
    rows, cols = grad_out.shape
    n_seq, n_ch = lax.axis_size("seq"), lax.axis_size("ch")
    basis = half_bin_basis(rows)
    forward = bf16(basis)
    inverse = bf16(basis.T / rows)
    all_rows = lax.all_gather(projection, "seq", axis=0, tiled=True)
    mirror = [(j, n_ch - 1 - j) for j in range(n_ch)]
    later = lax.ppermute(grad_out, "seq", [(i + 1, i) for i in range(n_seq - 1)])
    earlier = lax.ppermute(grad_out, "seq", [(i, i + 1) for i in range(n_seq - 1)])
    mirror_taps = lax.ppermute(filter_taps, "ch", mirror)[:, ::-1]

    def spectrum(block):
        return split(jnp.dot(forward, block, preferred_element_type=jnp.float32))

    sign = jnp.asarray(np.where(np.arange(rows) % 2 == 0, 1.0, -1.0).astype(np.float32))[:, None]
    here_r, here_i = spectrum(grad_out)
    next_r, next_i = spectrum(later)
    prev_r, prev_i = spectrum(earlier)
    in_r, in_i = spectrum(saved_in)
    tap_r, tap_i = spectrum(filter_taps)
    mir_r, mir_i = spectrum(mirror_taps)
    up_r, up_i = here_r + sign * next_i, here_i - sign * next_r
    dn_r, dn_i = here_r - sign * prev_i, here_i + sign * prev_r
    conv_r = up_r * tap_r + up_i * tap_i + dn_r * mir_r - dn_i * mir_i
    conv_i = up_i * tap_r - up_r * tap_i + dn_r * mir_i + dn_i * mir_r
    pos_r, pos_i = in_r * up_r + in_i * up_i, in_r * up_i - in_i * up_r
    neg_r, neg_i = in_r * dn_r + in_i * dn_i, in_i * dn_r - in_r * dn_i

    def back(real, imag):
        packed = jnp.concatenate([real, imag], axis=0).astype(jnp.bfloat16)
        return jnp.dot(inverse, packed, preferred_element_type=jnp.float32)

    conv_sum = back(conv_r, conv_i)
    grad_conv = (conv_sum + skip_gain[None, :] * grad_out.astype(jnp.float32)).astype(jnp.bfloat16)
    partial_value = lax.dot_general(
        grad_conv, all_rows, (((1,), (1,)), ((), ())), preferred_element_type=jnp.float32
    )
    grad_in = lax.psum_scatter(
        partial_value.astype(jnp.bfloat16), "ch", scatter_dimension=1, tiled=True
    )
    positive = lax.psum_scatter(back(pos_r, pos_i), "seq", scatter_dimension=0, tiled=True)
    negative = lax.psum_scatter(back(neg_r, neg_i), "seq", scatter_dimension=0, tiled=True)
    mirrored = lax.ppermute(negative, "ch", mirror)[:, ::-1]
    filter_grad = (positive + mirrored) * (1.0 / math.sqrt(rows * n_seq))
    return (grad_in, filter_grad)


def solution(mesh):
    placed = (P("seq", "ch"), P("seq", "ch"), P(None, "ch"), P("ch"), P("seq", "ch"))
    return jax.shard_map(
        body,
        mesh=mesh,
        in_specs=placed,
        out_specs=(P("seq", "ch"), P("seq", "ch")),
        check_vma=False,
    )
```

time: 1020 us -> 785 us (0.77)
  the two profiles are of different devices: /device:TPU:1 before, /device:TPU:8 now
where the time goes in v1:
time: 785 us; the launch traced here: 784 us
  waiting for transfers between devices  716 us (91%)
  starting transfers between devices  30.4 us (4%)
  matrix products  16.4 us (2%)
  between operations  14.6 us (2%)
    unnamed x4, waiting for transfers between devices  499 us
    reduce_scatter x1, waiting for transfers between devices, body(): lax.psum_scatter(partial_value.astype(jnp.bfloat16), 'ch', scatter_dimens...  115 us
    all_gather x1, waiting for transfers between devices, body(): all_rows = lax.all_gather(projection, 'seq', axis=0, tiled=True)  94.4 us
  transfers between devices with their start and end apart: 7, of which 5 were waited for; matrix products, arithmetic and copies ran while one was open for 3% of the time, Pallas kernels for 0%

profile of v1, /device:TPU:8, one launch (start us, length us, event | category | flops | bytes accessed | tf_op | source)
XLA Modules:
  0.0 784.2 jit_solution(5551402973084646898)
XLA Ops:
  7.2 0.7 all-gather.2.cloned.1.call-update
  8.0 10.3 %collective-permute-start = (bf16[256,512]{1,0:T(8,128)(2,1)}, bf16[256,512]{1,0:T(8,128)(2,1)S(1)}, u32[]{:S(2)}, u32[]{:S(2)}) collective-permute-start(bf16[256,512]{1,0:T(8,128)(2,1)} %param.8), channel_id=1, source_target_pairs={{8,0},{16,8},{24,16},{32,24},{40,32},{48,40},{56,48},{64,56},{72,6... | collective-permute-start | bytes 786440 | tf_op jit(solution)/shard_map/ppermute | solution.py:34
  18.3 1.9 collective-permute-start.1
  20.2 9.9 %collective-permute-start.2 = (bf16[256,512]{1,0:T(8,128)(2,1)}, bf16[256,512]{1,0:T(8,128)(2,1)S(1)}, u32[]{:S(2)}, u32[]{:S(2)}) collective-permute-start(bf16[256,512]{1,0:T(8,128)(2,1)} %param.10), channel_id=1, source_target_pairs={{0,7},{1,6},{2,5},{3,4},{4,3},{5,2},{6,1},{7,0},{8,15},{9,14},{10,... | collective-permute-start | bytes 786440 | tf_op jit(solution)/shard_map/ppermute | solution.py:36
  30.1 1.3 fusion.16
  31.5 2.3 fusion.18
  33.8 1.2 fusion.21
  36.0 0.4 fusion.12
  36.4 0.4 fusion.11
  36.8 1.2 fusion.2
  38.0 1.2 fusion.3
  39.6 0.8 rev.6
  40.7 1.0 copy-done.2
  41.7 1.6 fusion.15
  43.3 94.4 %all-gather.2.cloned.1.call-done = bf16[4096,512]{1,0:T(8,128)(2,1)} async-done(((bf16[64,512]{1,0:T(8,128)(2,1)}), bf16[4096,512]{1,0:T(8,128)(2,1)}) %all-gather.2.cloned.1.call-update) | async-done | bytes 4194320 | tf_op jit(solution)/shard_map/all_gather | solution.py:32
  137.7 5.8 convolution_convert_fusion
  143.6 1.3 dynamic-slice
  145.5 498.3 %all-reduce.5.cloned.1.call-done = (f32[256,512]{0,1:T(8,128)}, f32[256,512]{0,1:T(8,128)}) async-done(((f32[256,512]{0,1:T(8,128)}, f32[256,512]{0,1:T(8,128)}), (f32[256,512]{0,1:T(8,128)}, f32[256,512]{0,1:T(8,128)})) %all-reduce.5.cloned.1.call-update) | async-done | bytes 1048592
  643.8 1.1 constant_dynamic-slice_fusion
  644.9 8.2 %collective-permute-start.3 = (f32[4,512]{0,1:T(8,128)S(1)}, f32[4,512]{0,1:T(8,128)S(1)}, u32[]{:S(2)}, u32[]{:S(2)}) collective-permute-start(f32[4,512]{0,1:T(8,128)S(1)} %constant_dynamic-slice_fusion), channel_id=1, source_target_pairs={{0,7},{1,6},{2,5},{3,4},{4,3},{5,2},{6,1},{7,0},{8,15},{9,14},{10,... | collective-permute-start | bytes 24584 | tf_op jit(solution)/shard_map/ppermute | solution.py:69
  653.0 8.2 %collective-permute-done.3 = f32[4,512]{0,1:T(8,128)S(1)} collective-permute-done((f32[4,512]{0,1:T(8,128)S(1)}, f32[4,512]{0,1:T(8,128)S(1)}, u32[]{:S(2)}, u32[]{:S(2)}) %collective-permute-start.3) | collective-permute-done | bytes 8224 | tf_op jit(solution)/shard_map/ppermute | solution.py:69
  661.3 1.1 fusion.13
  662.4 0.7 copy.11
  663.1 114.6 %reduce-scatter.4.cloned.1.call-done = bf16[256,512]{1,0:T(8,128)(2,1)} async-done(((bf16[256,4096]{1,0:T(8,128)(2,1)}), bf16[256,512]{1,0:T(8,128)(2,1)}) %reduce-scatter.4.cloned.1.call-update) | async-done | bytes 262160 | tf_op jit(solution)/shard_map/reduce_scatter | solution.py:64
  (26 shorter events, 1.7 us)
Async XLA Ops:
  7.2 26.6 %copy-start = (bf16[256,512]{1,0:T(8,128)(2,1)S(1)}, bf16[256,512]{1,0:T(8,128)(2,1)}, u32[]{:S(2)}) copy-start(bf16[256,512]{1,0:T(8,128)(2,1)} %param.9) | copy-start | bytes 786436
  7.2 27.9 %copy-start.1 = (bf16[512,256]{1,0:T(8,128)(2,1)S(1)}, bf16[512,256]{1,0:T(8,128)(2,1)}, u32[]{:S(2)}) copy-start(bf16[512,256]{1,0:T(8,128)(2,1)} %constant.8.clone) | copy-start | bytes 786436
  7.2 28.5 %copy-start.6 = (f32[256]{0:T(256)S(1)}, f32[256]{0:T(256)}, u32[]{:S(2)}) copy-start(f32[256]{0:T(256)} %constant.10.clone) | copy-start | bytes 3076
  7.2 130.5 %all-gather.2.cloned.1.call-start = ((), (), s32[]{:S(2)}) async-start(), calls=%async_computation.1 | async-start | bytes 4259840 | tf_op jit(solution)/shard_map/all_gather | solution.py:32
  7.9 635.8 %all-reduce.5.cloned.1.call-start = ((), (), s32[]{:S(2)}) async-start(), calls=%async_computation.3 | async-start | bytes 2097152
  8.0 27.1 %collective-permute-start = (bf16[256,512]{1,0:T(8,128)(2,1)}, bf16[256,512]{1,0:T(8,128)(2,1)S(1)}, u32[]{:S(2)}, u32[]{:S(2)}) collective-permute-start(bf16[256,512]{1,0:T(8,128)(2,1)} %param.8), channel_id=1, source_target_pairs={{8,0},{16,8},{24,16},{32,24},{40,32},{48,40},{56,48},{64,56},{72,6... | collective-permute-start | bytes 786440 | tf_op jit(solution)/shard_map/ppermute | solution.py:34
  18.3 17.1 %collective-permute-start.1 = (bf16[256,512]{1,0:T(8,128)(2,1)}, bf16[256,512]{1,0:T(8,128)(2,1)S(1)}, u32[]{:S(2)}, u32[]{:S(2)}) collective-permute-start(bf16[256,512]{1,0:T(8,128)(2,1)} %param.8), channel_id=1, source_target_pairs={{0,8},{8,16},{16,24},{24,32},{32,40},{40,48},{48,56},{56,64},{64,7... | collective-permute-start | bytes 786440 | tf_op jit(solution)/shard_map/ppermute | solution.py:35
  20.2 19.4 %collective-permute-start.2 = (bf16[256,512]{1,0:T(8,128)(2,1)}, bf16[256,512]{1,0:T(8,128)(2,1)S(1)}, u32[]{:S(2)}, u32[]{:S(2)}) collective-permute-start(bf16[256,512]{1,0:T(8,128)(2,1)} %param.10), channel_id=1, source_target_pairs={{0,7},{1,6},{2,5},{3,4},{4,3},{5,2},{6,1},{7,0},{8,15},{9,14},{10,... | collective-permute-start | bytes 786440 | tf_op jit(solution)/shard_map/ppermute | solution.py:36
  35.0 0.9 copy-start.4
  35.7 1.1 copy-start.3
  38.0 99.7 %copy-start.5 = (f32[512]{0:T(512)S(1)}, f32[512]{0:T(512)}, u32[]{:S(2)}) copy-start(f32[512]{0:T(512)} %param.11) | copy-start | bytes 6148
  39.2 738.5 %reduce-scatter.4.cloned.1.call-start = ((), (), s32[]{:S(2)}) async-start(), calls=%async_computation.2 | async-start | bytes 2359296 | tf_op jit(solution)/shard_map/reduce_scatter | solution.py:64
  40.7 1.0 copy-start.2
  644.9 16.4 %collective-permute-start.3 = (f32[4,512]{0,1:T(8,128)S(1)}, f32[4,512]{0,1:T(8,128)S(1)}, u32[]{:S(2)}, u32[]{:S(2)}) collective-permute-start(f32[4,512]{0,1:T(8,128)S(1)} %constant_dynamic-slice_fusion), channel_id=1, source_target_pairs={{0,7},{1,6},{2,5},{3,4},{4,3},{5,2},{6,1},{7,0},{8,15},{9,14},{10,... | collective-permute-start | bytes 24584 | tf_op jit(solution)/shard_map/ppermute | solution.py:69
Sparse Core Ops, SparseCore 0:
  10.2 127.4 all-gather.1
  140.7 503.0 all-reduce.4
  649.7 127.9 reduce-scatter.3

commit v2 on v1

v2 whole, which is shorter than its diff:
```python
import math

import jax
import jax.numpy as jnp
import ml_dtypes
import numpy as np
from jax import lax
from jax.experimental import pallas as pl
from jax.experimental.pallas import tpu as pltpu
from jax.sharding import PartitionSpec as P

NY, NZ, NX = 4, 8, 4
ROWS, COLS = 256, 512
F32, BF16 = jnp.float32, jnp.bfloat16
OFFSETS = (0, -1, 1, -2, 2, -3, 3, 4)


def half_bin_basis(rows):
    angle = np.pi * np.outer(np.arange(rows) + 0.5, np.arange(rows)) / rows
    return np.concatenate([np.cos(angle), -np.sin(angle)], axis=0)


def lag_order():
    core, z, y, r = np.meshgrid(np.arange(2), np.arange(NZ), np.arange(NY), np.arange(4), indexing="ij")
    return (((y * NZ + z) * 2 + core) * 4 + r).reshape(-1)


def dot(a, b):
    return jnp.dot(a, b, preferred_element_type=F32)


def kernel(
    g_ref, x_ref, f_ref, skip_ref, p_ref, fwd_ref, inv_ref, lag_ref,
    out_ref, fg_ref,
    halo, mt, pg, sx, rx, ysend, yrecv, gc, rev,
    s_here, s_in, s_tap, s_next, s_prev, s_mir, q_conv, q_pos, q_neg,
    lags, kbuf, half_sum, zbuf, ysum, ypos, yneg,
    tap_ss, tap_rs, halo_ss, halo_rs, py_ss, py_rs, ring_ss, ring_rs, sib_ss, sib_rs, last_ss, last_rs,
    xs_ss, xs_rs, yh_ss, yh_rs, k_ss, k_rs, z_ss, z_rs, y_ss, y_rs,
):
    seq, ch = lax.axis_index("seq"), lax.axis_index("ch")
    y, z, k = seq // 16, (seq // 2) % NZ, seq % 2
    half, x = ch // NX, ch % NX

    def at(y_, z_, k_, half_, x_):
        return ((y_ * NZ + z_) * 2 + k_, half_ * NX + x_)

    def send(src, dst, ssem, rsem, device):
        return pltpu.make_async_remote_copy(
            src_ref=src, dst_ref=dst, send_sem=ssem, recv_sem=rsem,
            device_id=device, device_id_type=pl.DeviceIdType.MESH,
        )

    me = (seq, ch)
    later = ((seq + 1) % 64, ch)
    earlier = ((seq + 63) % 64, ch)
    sibling = at(y, z, 1 - k, half, x)
    pair = z + 1 - 2 * (z % 2)
    other_half = at(y, z, k, 1 - half, x)

    def along_y(d):
        return at((y + d) % NY, z, k, half, x)

    def along_z(d):
        return at(y, (z + d + NZ) % NZ, k, half, x)

    def along_x(d):
        return at(y, z, k, half, (x + d) % NX)

    def mirror(d):
        return at((y + d) % NY, z, k, 1 - half, NX - 1 - x)

    friends = [along_z(d) for d in range(1, NZ)] + [along_y(d) for d in range(1, NY)]
    friends += [along_x(d) for d in range(1, NX)] + [mirror(d) for d in range(NY)]
    friends += [later, earlier, sibling, other_half, at(y, pair, k, half, x), at(y, pair, 1 - k, half, x)]
    barrier = pltpu.get_barrier_semaphore()
    for friend in friends:
        pl.semaphore_signal(barrier, inc=1, device_id=friend, device_id_type=pl.DeviceIdType.MESH)
    pl.semaphore_wait(barrier, len(friends))

    pending = []

    def go(copy):
        copy.start()
        pending.append(copy)

    mine = (z % 2) * 2 + k
    go(send(f_ref.at[pl.ds(pl.multiple_of(mine * 64, 64), 64)], mt.at[mine], tap_ss.at[0], tap_rs.at[0], mirror(0)))
    go(send(g_ref, halo.at[0], halo_ss.at[0], halo_rs.at[0], earlier))
    go(send(g_ref, halo.at[1], halo_ss.at[1], halo_rs.at[1], later))
    for d in range(1, NY):
        go(send(p_ref, pg.at[y, z, k], py_ss.at[d - 1], py_rs.at[d - 1], along_y(d)))

    def forward(way, step, dy, src):
        sign = 1 - 2 * way
        origin = (z - sign * (step - 1) + NZ) % NZ
        slot = pg.at[(y + dy) % NY, origin, k]
        go(send(slot if src is None else src, slot, ring_ss.at[way, step - 1, dy], ring_rs.at[way, step - 1, dy], along_z(sign)))

    forward(0, 1, 0, p_ref)
    forward(1, 1, 0, p_ref)
    pg[y, z, k] = p_ref[...]

    fwd = fwd_ref[...]
    s_here[...] = dot(fwd, g_ref[...])
    s_in[...] = dot(fwd, x_ref[...])
    s_tap[...] = dot(fwd, f_ref[...])
    row = lax.broadcasted_iota(jnp.int32, (COLS, COLS), 0)
    col = lax.broadcasted_iota(jnp.int32, (COLS, COLS), 1)
    rev[...] = jnp.where(row + col == COLS - 1, 1.0, 0.0).astype(BF16)

    send(mt.at[mine], mt.at[mine], tap_ss.at[0], tap_rs.at[0], me).wait_recv()
    group = ((z, 1 - k), (pair, k), (pair, 1 - k))
    for i, (z_, k_) in enumerate(group):
        go(send(mt.at[mine], mt.at[mine], tap_ss.at[1 + i], tap_rs.at[1 + i], at(y, z_, k_, half, x)))

    for d in range(1, NY):
        slot = pg.at[(y + NY - d) % NY, z, k]
        send(slot, slot, py_ss.at[d - 1], py_rs.at[d - 1], me).wait_recv()
        forward(0, 1, NY - d, None)
        forward(1, 1, NY - d, None)

    def to_sibling(number):
        slot = pg.at[:, (z + OFFSETS[number] + NZ) % NZ, k]
        go(send(slot, slot, sib_ss.at[number], sib_rs.at[number], sibling))

    to_sibling(0)

    for i in range(2):
        send(halo.at[i], halo.at[i], halo_ss.at[i], halo_rs.at[i], me).wait_recv()
    s_next[...] = dot(fwd, halo[0])
    s_prev[...] = dot(fwd, halo[1])
    for i, (z_, k_) in enumerate(group):
        slot = mt.at[(z_ % 2) * 2 + k_]
        send(slot, slot, tap_ss.at[1 + i], tap_rs.at[1 + i], me).wait_recv()
    mirror_taps = dot(mt[...].reshape(ROWS, COLS), rev[...]).astype(BF16)
    s_mir[...] = dot(fwd, mirror_taps)

    def serve(step):
        for way in range(2):
            sign = 1 - 2 * way
            origin = (z - sign * step + NZ) % NZ
            for dy in ((0, 3, 2, 1) if step < 4 else ((0, 3) if way == 0 else (2, 1))):
                slot = pg.at[(y + dy) % NY, origin, k]
                send(slot, slot, ring_ss.at[way, step - 1, dy], ring_rs.at[way, step - 1, dy], me).wait_recv()
                if step < 3 or (step == 3 and dy in ((0, 3) if way == 0 else (2, 1))):
                    forward(way, step + 1, dy, None)
                if step == 4:
                    go(send(slot, slot, last_ss.at[dy], last_rs.at[dy], sibling))
            if step < 4:
                to_sibling(2 * step - 1 + way)

    serve(1)

    ahead = jnp.where(seq < 63, 1.0, 0.0)
    behind = jnp.where(seq > 0, 1.0, 0.0)
    even = lax.broadcasted_iota(jnp.int32, (16, COLS), 0) % 2 == 0
    up_sign = jnp.where(even, ahead, -ahead)
    dn_sign = jnp.where(even, behind, -behind)

    @pl.loop(0, ROWS // 16)
    def _(i):
        re = pl.ds(pl.multiple_of(i * 16, 16), 16)
        im = pl.ds(pl.multiple_of(ROWS + i * 16, 16), 16)
        here_r, here_i = s_here[re, :], s_here[im, :]
        up_r, up_i = here_r + up_sign * s_next[im, :], here_i - up_sign * s_next[re, :]
        dn_r, dn_i = here_r - dn_sign * s_prev[im, :], here_i + dn_sign * s_prev[re, :]
        tap_r, tap_i, mir_r, mir_i = s_tap[re, :], s_tap[im, :], s_mir[re, :], s_mir[im, :]
        in_r, in_i = s_in[re, :], s_in[im, :]
        q_conv[re, :] = (up_r * tap_r + up_i * tap_i + dn_r * mir_r - dn_i * mir_i).astype(BF16)
        q_conv[im, :] = (up_i * tap_r - up_r * tap_i + dn_r * mir_i + dn_i * mir_r).astype(BF16)
        q_pos[re, :] = (in_r * up_r + in_i * up_i).astype(BF16)
        q_pos[im, :] = (in_r * up_i - in_i * up_r).astype(BF16)
        q_neg[re, :] = (in_r * dn_r + in_i * dn_i).astype(BF16)
        q_neg[im, :] = (in_i * dn_r - in_r * dn_i).astype(BF16)

    conv = dot(inv_ref[...], q_conv[...])
    gc[...] = (conv + skip_ref[...] * g_ref[...].astype(F32)).astype(BF16)

    def x_copy(number, part):
        z_ = (z + OFFSETS[number] + NZ) % NZ
        to = 2 * part + z_ // 4
        d = (to - x + NX) % NX
        index = (d + NX - 1) % NX
        copy = send(
            sx.at[part, z_], rx.at[index, z_ % 4], xs_ss.at[number, part], xs_rs.at[index, z_ % 4], along_x(d)
        )
        return d != 0, copy

    def multiply(number):
        z_ = (z + OFFSETS[number] + NZ) % NZ
        if number < 7:
            slot = pg.at[:, z_, 1 - k]
            send(slot, slot, sib_ss.at[number], sib_rs.at[number], me).wait_recv()
        else:
            for dy in range(NY):
                slot = pg.at[(y + dy) % NY, z_, 1 - k]
                send(slot, slot, last_ss.at[dy], last_rs.at[dy], me).wait_recv()

        @pl.loop(0, NY)
        def _(y_):
            block = pg[y_, z_].reshape(128, COLS)
            part = lax.dot_general(gc[...], block, (((1,), (1,)), ((), ())), preferred_element_type=F32)
            sx[y_ % 2, z_, y_ // 2] = part.astype(BF16)

        for part in range(2):
            remote, copy = x_copy(number, part)

            @pl.when(remote)
            def _():
                copy.start()

    def chunk_sum(z_, which):
        total = sx[x // 2, z_, which].astype(F32)
        for index in range(NX - 1):
            total = total + rx[index, z_ % 4, which].astype(F32)
        return total

    def yh_copy(zq):
        return send(ysend.at[zq], yrecv.at[zq], yh_ss.at[zq], yh_rs.at[zq], other_half)

    def pass_half(number):
        z_ = (z + OFFSETS[number] + NZ) % NZ

        @pl.when(z_ // 4 == x % 2)
        def _():
            zq = z_ % 4
            for index in range(NX - 1):
                slot = rx.at[index, zq]
                send(slot, slot, xs_ss.at[0, 0], xs_rs.at[index, zq], me).wait_recv()
            ysend[zq] = chunk_sum(z_, 1 - half).astype(BF16)
            yh_copy(zq).start()

    multiply(0)

    lags[0] = dot(lag_ref[...], q_pos[...]).astype(BF16).reshape(2, NZ, 16, COLS)
    negative = dot(q_neg[...], rev[...]).astype(BF16)
    lags[1] = dot(lag_ref[...], negative).astype(BF16).reshape(2, NZ, 16, COLS)
    go(send(lags.at[:, 1 - k], kbuf, k_ss.at[0], k_rs.at[0], sibling))

    multiply(1)
    multiply(2)
    serve(2)
    send(kbuf, kbuf, k_ss.at[0], k_rs.at[0], me).wait_recv()
    for i in range(2):
        for z_ in range(NZ):
            half_sum[z_, i] = (lags[i, k, z_].astype(F32) + kbuf[i, z_].astype(F32)).astype(BF16)
    for d in range(1, NZ):
        go(send(half_sum.at[(z + d) % NZ], zbuf.at[d - 1], z_ss.at[d - 1], z_rs.at[d - 1], along_z(d)))
    pass_half(0)
    multiply(3)
    multiply(4)
    pass_half(1)
    pass_half(2)
    serve(3)
    multiply(5)
    multiply(6)
    for d in range(1, NZ):
        slot = zbuf.at[d - 1]
        send(slot, slot, z_ss.at[d - 1], z_rs.at[d - 1], me).wait_recv()
    for i in range(2):
        total = half_sum[z, i].astype(F32)
        for d in range(1, NZ):
            total = total + zbuf[d - 1, i].astype(F32)
        for y_ in range(NY):
            ysum[i, y_, 0:4] = total[4 * y_ : 4 * y_ + 4]
    for d in range(NY):
        to = (y + d) % NY
        go(send(ysum.at[1, to], yneg.at[d], y_ss.at[1, d], y_rs.at[1, d], mirror(d)))
        if d > 0:
            go(send(ysum.at[0, to], ypos.at[d - 1], y_ss.at[0, d], y_rs.at[0, d], along_y(d)))
    pass_half(3)
    pass_half(4)
    serve(4)
    multiply(7)
    pass_half(5)
    pass_half(6)

    total = ysum[0, y, 0:4]
    for d in range(NY):
        send(yneg.at[d], yneg.at[d], y_ss.at[1, d], y_rs.at[1, d], me).wait_recv()
        total = total + yneg[d, 0:4]
        if d > 0:
            send(ypos.at[d - 1], ypos.at[d - 1], y_ss.at[0, d], y_rs.at[0, d], me).wait_recv()
            total = total + ypos[d - 1, 0:4]
    fg_ref[...] = total * (1.0 / math.sqrt(16384))
    pass_half(7)

    for number in range(8):
        z_ = (z + OFFSETS[number] + NZ) % NZ

        @pl.when(z_ // 4 == x % 2)
        def _():
            zq = z_ % 4
            yh_copy(zq).wait_recv()
            value = chunk_sum(z_, half) + yrecv[zq].astype(F32)
            out_ref[:, pl.ds(pl.multiple_of(zq * 128, 128), 128)] = value.astype(BF16)

    for copy in pending:
        copy.wait_send()
    for zq in range(4):
        yh_copy(zq).wait_send()
    for number in range(8):
        for part in range(2):
            remote, copy = x_copy(number, part)

            @pl.when(remote)
            def _():
                copy.wait_send()


def body(grad_out, saved_in, filter_taps, skip_gain, projection):
    basis = half_bin_basis(ROWS)
    inverse = basis.T / ROWS

    def bf16(values):
        return jnp.asarray(values.astype(ml_dtypes.bfloat16))

    vmem, dma = pltpu.VMEM, pltpu.SemaphoreType.DMA
    square = vmem((2 * ROWS, COLS), F32)
    packed = vmem((2 * ROWS, COLS), BF16)
    scratch = [
        vmem((2, ROWS, COLS), BF16),
        vmem((4, 64, COLS), BF16),
        vmem((NY, NZ, 2, 64, COLS), BF16),
        vmem((2, NZ, 2, ROWS, 128), BF16),
        vmem((NX - 1, 4, 2, ROWS, 128), BF16),
        vmem((4, ROWS, 128), BF16),
        vmem((4, ROWS, 128), BF16),
        vmem((ROWS, COLS), BF16),
        vmem((COLS, COLS), BF16),
        square, square, square, square, square, square, packed, packed, packed,
        vmem((2, 2, NZ, 16, COLS), BF16),
        vmem((2, NZ, 16, COLS), BF16),
        vmem((NZ, 2, 16, COLS), BF16),
        vmem((NZ - 1, 2, 16, COLS), BF16),
        vmem((2, NY, 8, COLS), F32),
        vmem((NY - 1, 8, COLS), F32),
        vmem((NY, 8, COLS), F32),
        dma((4,)), dma((4,)), dma((2,)), dma((2,)), dma((3,)), dma((3,)),
        dma((2, 4, 4)), dma((2, 4, 4)), dma((7,)), dma((7,)), dma((4,)), dma((4,)),
        dma((8, 2)), dma((3, 4)), dma((4,)), dma((4,)), dma((1,)), dma((1,)),
        dma((7,)), dma((7,)), dma((2, 4)), dma((2, 4)),
    ]
    return pl.pallas_call(
        kernel,
        out_shape=(jax.ShapeDtypeStruct((ROWS, COLS), BF16), jax.ShapeDtypeStruct((4, COLS), F32)),
        in_specs=[pl.BlockSpec(memory_space=vmem)] * 8,
        out_specs=(pl.BlockSpec(memory_space=vmem), pl.BlockSpec(memory_space=vmem)),
        scratch_shapes=scratch,
        compiler_params=pltpu.CompilerParams(
            collective_id=0, has_side_effects=True, vmem_limit_bytes=48 << 20
        ),
        name="conv_backward",
    )(
        grad_out, saved_in, filter_taps, skip_gain.reshape(1, COLS), projection,
        bf16(basis), bf16(inverse), bf16(inverse[lag_order()]),
    )


def solution(mesh):
    placed = (P("seq", "ch"), P("seq", "ch"), P(None, "ch"), P("ch"), P("seq", "ch"))
    return jax.shard_map(
        body,
        mesh=mesh,
        in_specs=placed,
        out_specs=(P("seq", "ch"), P("seq", "ch")),
        check_vma=False,
    )
```

time: 785 us -> 85 us (0.11)
  the two profiles are of different devices: /device:TPU:8 before, /device:TPU:71 now
where the time goes in v2:
time: 85 us; the launch traced here: 84.6 us
  Pallas kernels  75.4 us (89%)
  local copies, waits for them, and re-layouts  8.51 us (10%)
    pallas_call x1, Pallas kernels, body(): pl.pallas_call(kernel, out_shape=(jax.ShapeDtypeStruct((ROWS, COLS), BF16...  75.4 us
    unnamed x18, local copies, waits for them, and re-layouts  8.51 us

profile of v2, /device:TPU:71, one launch (start us, length us, event | category | flops | bytes accessed | tf_op | source)
XLA Modules:
  0.0 84.6 jit_solution(16897343075669405389)
XLA Ops:
  0.6 0.0 copy-start
  0.6 0.9 %copy-done = bf16[256,512]{1,0:T(8,128)(2,1)S(1)} copy-done((bf16[256,512]{1,0:T(8,128)(2,1)S(1)}, bf16[256,512]{1,0:T(8,128)(2,1)}, u32[]{:S(2)}) %copy-start) | copy-done | bytes 262168
  1.6 0.0 copy-start.1
  1.6 0.9 %copy-done.1 = bf16[256,512]{1,0:T(8,128)(2,1)S(1)} copy-done((bf16[256,512]{1,0:T(8,128)(2,1)S(1)}, bf16[256,512]{1,0:T(8,128)(2,1)}, u32[]{:S(2)}) %copy-start.1) | copy-done | bytes 262168
  2.5 0.0 copy-start.2
  2.5 0.9 %copy-done.2 = bf16[256,512]{1,0:T(8,128)(2,1)S(1)} copy-done((bf16[256,512]{1,0:T(8,128)(2,1)S(1)}, bf16[256,512]{1,0:T(8,128)(2,1)}, u32[]{:S(2)}) %copy-start.2) | copy-done | bytes 262168
  3.5 0.0 copy-start.3
  3.5 0.9 %copy-done.3 = bf16[256,512]{1,0:T(8,128)(2,1)S(1)} copy-done((bf16[256,512]{1,0:T(8,128)(2,1)S(1)}, bf16[256,512]{1,0:T(8,128)(2,1)}, u32[]{:S(2)}) %copy-start.3) | copy-done | bytes 262168
  4.4 0.0 copy-start.4
  4.4 0.9 %copy-done.4 = bf16[256,512]{1,0:T(8,128)(2,1)S(1)} copy-done((bf16[256,512]{1,0:T(8,128)(2,1)S(1)}, bf16[256,512]{1,0:T(8,128)(2,1)}, u32[]{:S(2)}) %copy-start.4) | copy-done | bytes 262168
  5.4 0.0 copy-start.5
  5.4 0.9 %copy-done.5 = bf16[512,256]{1,0:T(8,128)(2,1)S(1)} copy-done((bf16[512,256]{1,0:T(8,128)(2,1)S(1)}, bf16[512,256]{1,0:T(8,128)(2,1)}, u32[]{:S(2)}) %copy-start.5) | copy-done | bytes 262168
  6.3 0.0 copy-start.6
  6.3 0.8 copy-done.6
  7.2 0.0 copy-start.7
  7.2 0.7 copy-done.7
  7.9 75.4 %conv_backward.1 = (bf16[256,512]{1,0:T(8,128)(2,1)S(1)}, f32[4,512]{1,0:T(4,128)S(1)}) custom-call(bf16[256,512]{1,0:T(8,128)(2,1)S(1)} %copy-done, bf16[256,512]{1,0:T(8,128)(2,1)S(1)} %copy-done.1, bf16[256,512]{1,0:T(8,128)(2,1)S(1)} %copy-done.2, f32[1,512]{1,0:T(1,128)S(1)} %bitcast.1, bf16[64,512]{1,0:T(8,128)(2,1)S(1)} %copy-done.6, ...), custom_call_target="tpu_custom_call" | custom-call | tf_op jit(solution)/shard_map/conv_backward/pallas_call | solution.py:345
  83.3 0.7 copy.12
  84.0 0.6 copy.13
Async XLA Ops:
  0.6 1.0 %copy-start = (bf16[256,512]{1,0:T(8,128)(2,1)S(1)}, bf16[256,512]{1,0:T(8,128)(2,1)}, u32[]{:S(2)}) copy-start(bf16[256,512]{1,0:T(8,128)(2,1)} %g_ref.1) | copy-start | bytes 786436
  1.6 0.9 %copy-start.1 = (bf16[256,512]{1,0:T(8,128)(2,1)S(1)}, bf16[256,512]{1,0:T(8,128)(2,1)}, u32[]{:S(2)}) copy-start(bf16[256,512]{1,0:T(8,128)(2,1)} %x_ref.1) | copy-start | bytes 786436
  2.5 0.9 %copy-start.2 = (bf16[256,512]{1,0:T(8,128)(2,1)S(1)}, bf16[256,512]{1,0:T(8,128)(2,1)}, u32[]{:S(2)}) copy-start(bf16[256,512]{1,0:T(8,128)(2,1)} %f_ref.1) | copy-start | bytes 786436
  3.5 0.9 %copy-start.3 = (bf16[256,512]{1,0:T(8,128)(2,1)S(1)}, bf16[256,512]{1,0:T(8,128)(2,1)}, u32[]{:S(2)}) copy-start(bf16[256,512]{1,0:T(8,128)(2,1)} %constant.8.clone.lag_ref) | copy-start | bytes 786436
  4.4 0.9 %copy-start.4 = (bf16[256,512]{1,0:T(8,128)(2,1)S(1)}, bf16[256,512]{1,0:T(8,128)(2,1)}, u32[]{:S(2)}) copy-start(bf16[256,512]{1,0:T(8,128)(2,1)} %constant.7.clone.inv_ref) | copy-start | bytes 786436
  5.4 0.9 %copy-start.5 = (bf16[512,256]{1,0:T(8,128)(2,1)S(1)}, bf16[512,256]{1,0:T(8,128)(2,1)}, u32[]{:S(2)}) copy-start(bf16[512,256]{1,0:T(8,128)(2,1)} %constant.6.clone.fwd_ref) | copy-start | bytes 786436
  6.3 0.8 copy-start.6
  7.2 0.7 copy-start.7

commit v3 on v2

v3 whole, which is shorter than its diff:
```python
import math

import jax
import jax.numpy as jnp
import ml_dtypes
import numpy as np
from jax import lax
from jax.experimental import pallas as pl
from jax.experimental.pallas import tpu as pltpu
from jax.sharding import PartitionSpec as P

NY, NZ, NX = 4, 8, 4
ROWS, COLS = 256, 512
F32, BF16 = jnp.float32, jnp.bfloat16
OFFSETS = (0, -1, 1, -2, 2, -3, 3, 4)


def half_bin_basis(rows):
    angle = np.pi * np.outer(np.arange(rows) + 0.5, np.arange(rows)) / rows
    return np.concatenate([np.cos(angle), -np.sin(angle)], axis=0)


def lag_order():
    core, y, z, r = np.meshgrid(np.arange(2), np.arange(NY), np.arange(NZ), np.arange(4), indexing="ij")
    return (((y * NZ + z) * 2 + core) * 4 + r).reshape(-1)


def dot(a, b):
    return jnp.dot(a, b, preferred_element_type=F32)


def kernel(
    g_hbm, x_hbm, f_hbm, skip_hbm, p_hbm, fwd_hbm, inv_hbm, lag_hbm,
    out_ref, fg_ref,
    g_ref, x_ref, f_ref, skip_ref, fwd_ref, inv_ref, lag_ref, in_sem,
    halo, mt, pg, sx, rx, ysend, yrecv, gc, rev,
    s_here, s_in, s_tap, s_next, s_prev, s_mir, q_conv, q_pos, q_neg,
    lags, kbuf, half_sum, ybuf, zsum, zpos, zneg,
    first_ss, tap_ss, tap_rs, halo_ss, halo_rs, py_ss, py_rs, ring_ss, ring_rs, sib_ss, sib_rs, last_ss, last_rs,
    xs_ss, xs_rs, yh_ss, yh_rs, k_ss, k_rs, y_ss, y_rs, z_ss, z_rs,
):
    seq, ch = lax.axis_index("seq"), lax.axis_index("ch")
    y, z, k = seq // 16, (seq // 2) % NZ, seq % 2
    half, x = ch // NX, ch % NX

    loads = [
        pltpu.make_async_copy(source, target, in_sem.at[i])
        for i, (source, target) in enumerate((
            (g_hbm, g_ref), (fwd_hbm, fwd_ref), (x_hbm, x_ref), (f_hbm, f_ref), (p_hbm, pg.at[y, z, k]),
            (inv_hbm, inv_ref), (lag_hbm, lag_ref), (skip_hbm, skip_ref),
        ))
    ]
    for load in loads:
        load.start()

    def at(y_, z_, k_, half_, x_):
        return ((y_ * NZ + z_) * 2 + k_, half_ * NX + x_)

    def send(src, dst, ssem, rsem, device):
        return pltpu.make_async_remote_copy(
            src_ref=src, dst_ref=dst, send_sem=ssem, recv_sem=rsem,
            device_id=device, device_id_type=pl.DeviceIdType.MESH,
        )

    me = (seq, ch)
    later = ((seq + 1) % 64, ch)
    earlier = ((seq + 63) % 64, ch)
    sibling = at(y, z, 1 - k, half, x)
    pair = z + 1 - 2 * (z % 2)
    other_half = at(y, z, k, 1 - half, x)

    def along_y(d):
        return at((y + d) % NY, z, k, half, x)

    def along_z(d):
        return at(y, (z + d + NZ) % NZ, k, half, x)

    def along_x(d):
        return at(y, z, k, half, (x + d) % NX)

    def mirror(d):
        return at(y, (z + d) % NZ, k, 1 - half, NX - 1 - x)

    friends = [along_z(d) for d in range(1, NZ)] + [along_y(d) for d in range(1, NY)]
    friends += [along_x(d) for d in range(1, NX)] + [mirror(d) for d in range(NZ)]
    friends += [later, earlier, sibling, other_half, at(y, pair, k, half, x), at(y, pair, 1 - k, half, x)]
    barrier = pltpu.get_barrier_semaphore()
    for friend in friends:
        pl.semaphore_signal(barrier, inc=1, device_id=friend, device_id_type=pl.DeviceIdType.MESH)
    source = at(3 * (1 - y // 2), z, k, 1 - half, NX - 1 - x)
    pl.semaphore_signal(barrier, inc=1, device_id=source, device_id_type=pl.DeviceIdType.MESH)
    serves = y % 3 == 0
    pl.semaphore_wait(barrier, len(friends) + jnp.where(serves, 2, 0))

    pending = []

    def go(copy):
        copy.start()
        pending.append(copy)

    mine = (z % 2) * 2 + k
    served = [
        send(
            f_hbm.at[pl.ds(pl.multiple_of(mine * 64, 64), 64)], mt.at[mine], first_ss.at[i], tap_rs.at[0],
            at(2 * (1 - y // 3) + i, z, k, 1 - half, NX - 1 - x),
        )
        for i in range(2)
    ]

    @pl.when(serves)
    def _():
        for copy in served:
            copy.start()

    go(send(g_hbm, halo.at[0], halo_ss.at[0], halo_rs.at[0], earlier))
    go(send(g_hbm, halo.at[1], halo_ss.at[1], halo_rs.at[1], later))
    def row_block(j):
        return (2 * (1 - half) + j) % NY

    def group_z(number):
        return (z + OFFSETS[number] + NZ) % NZ

    def hop(way, step, j):
        sign = 1 - 2 * way
        slot = pg.at[row_block(j), (z - sign * (step - 1) + NZ) % NZ, k]
        return send(slot, slot, ring_ss.at[way, step - 1, j], ring_rs.at[way, step - 1, j], along_z(sign))

    def arrived(way, step, j):
        slot = pg.at[row_block(j), (z - (1 - 2 * way) * step + NZ) % NZ, k]
        send(slot, slot, ring_ss.at[way, step - 1, j], ring_rs.at[way, step - 1, j], me).wait_recv()

    def to_sibling(phase, number):
        slot = pg.at[pl.ds(row_block(2 * phase), 2), group_z(number), k]
        go(send(slot, slot, sib_ss.at[phase, number], sib_rs.at[phase, number], sibling))

    def begin(phase):
        for j in (2 * phase, 2 * phase + 1):
            block = row_block(j)

            @pl.when(block != y)
            def _():
                slot = pg.at[block, z, k]
                send(slot, slot, py_ss.at[0], py_rs.at[block], me).wait_recv()
                hop(0, 1, j).start()
                hop(1, 1, j).start()

        to_sibling(phase, 0)

    own = (y + 2 + 2 * half) % NY

    def serve_own(step):
        for way in range(2):
            arrived(way, step, own)
            if step < 3:
                hop(way, step + 1, own).start()
            else:
                @pl.when(own % 2 == way)
                def _():
                    hop(way, 4, own).start()

    def serve(phase, step):
        for way in range(2):
            if step == 4:
                j = 2 * phase + way
                arrived(way, 4, j)
                slot = pg.at[row_block(j), group_z(7), k]
                go(send(slot, slot, last_ss.at[j], last_rs.at[j], sibling))
            else:
                for j in (2 * phase, 2 * phase + 1):
                    @pl.when(j != own)
                    def _():
                        arrived(way, step, j)
                        if step < 3 or j % 2 == way:
                            hop(way, step + 1, j).start()

                to_sibling(phase, 2 * step - 1 + way)

    for load in loads:
        load.wait()
    hop(0, 1, own).start()
    hop(1, 1, own).start()
    for d in range(1, NY):
        go(send(p_hbm, pg.at[y, z, k], py_ss.at[d - 1], py_rs.at[y], along_y(d)))
    fwd = fwd_ref[...]
    s_here[...] = dot(fwd, g_ref[...])
    s_in[...] = dot(fwd, x_ref[...])
    s_tap[...] = dot(fwd, f_ref[...])
    row = lax.broadcasted_iota(jnp.int32, (COLS, COLS), 0)
    col = lax.broadcasted_iota(jnp.int32, (COLS, COLS), 1)
    rev[...] = jnp.where(row + col == COLS - 1, 1.0, 0.0).astype(BF16)

    send(mt.at[mine], mt.at[mine], tap_ss.at[0], tap_rs.at[0], me).wait_recv()
    group = ((z, 1 - k), (pair, k), (pair, 1 - k))
    for i, (z_, k_) in enumerate(group):
        go(send(mt.at[mine], mt.at[mine], tap_ss.at[1 + i], tap_rs.at[1 + i], at(y, z_, k_, half, x)))

    serve_own(1)
    for i in range(2):
        send(halo.at[i], halo.at[i], halo_ss.at[i], halo_rs.at[i], me).wait_recv()
    s_next[...] = dot(fwd, halo[0])
    s_prev[...] = dot(fwd, halo[1])
    begin(0)
    begin(1)
    for i, (z_, k_) in enumerate(group):
        slot = mt.at[(z_ % 2) * 2 + k_]
        send(slot, slot, tap_ss.at[1 + i], tap_rs.at[1 + i], me).wait_recv()
    mirror_taps = dot(mt[...].reshape(ROWS, COLS), rev[...]).astype(BF16)
    s_mir[...] = dot(fwd, mirror_taps)
    serve_own(2)

    ahead = jnp.where(seq < 63, 1.0, 0.0)
    behind = jnp.where(seq > 0, 1.0, 0.0)
    even = lax.broadcasted_iota(jnp.int32, (16, COLS), 0) % 2 == 0
    up_sign = jnp.where(even, ahead, -ahead)
    dn_sign = jnp.where(even, behind, -behind)

    @pl.loop(0, ROWS // 16)
    def _(i):
        re = pl.ds(pl.multiple_of(i * 16, 16), 16)
        im = pl.ds(pl.multiple_of(ROWS + i * 16, 16), 16)
        here_r, here_i = s_here[re, :], s_here[im, :]
        up_r, up_i = here_r + up_sign * s_next[im, :], here_i - up_sign * s_next[re, :]
        dn_r, dn_i = here_r - dn_sign * s_prev[im, :], here_i + dn_sign * s_prev[re, :]
        tap_r, tap_i, mir_r, mir_i = s_tap[re, :], s_tap[im, :], s_mir[re, :], s_mir[im, :]
        in_r, in_i = s_in[re, :], s_in[im, :]
        q_conv[re, :] = (up_r * tap_r + up_i * tap_i + dn_r * mir_r - dn_i * mir_i).astype(BF16)
        q_conv[im, :] = (up_i * tap_r - up_r * tap_i + dn_r * mir_i + dn_i * mir_r).astype(BF16)
        q_pos[re, :] = (in_r * up_r + in_i * up_i).astype(BF16)
        q_pos[im, :] = (in_r * up_i - in_i * up_r).astype(BF16)
        q_neg[re, :] = (in_r * dn_r + in_i * dn_i).astype(BF16)
        q_neg[im, :] = (in_i * dn_r - in_r * dn_i).astype(BF16)

    conv = dot(inv_ref[...], q_conv[...])
    gc[...] = (conv + skip_ref[...] * g_ref[...].astype(F32)).T.astype(BF16)

    def x_copy(phase, number, part):
        z_ = group_z(number)
        d = (2 * part + z_ // 4 - x + NX) % NX
        index = (d + NX - 1) % NX
        copy = send(
            sx.at[phase, number, part], rx.at[phase, index, z_ % 4],
            xs_ss.at[phase, number, part], xs_rs.at[phase, index, z_ % 4], along_x(d),
        )
        return d != 0, copy

    def multiply(phase, number):
        z_ = group_z(number)
        if number < 7:
            slot = pg.at[pl.ds(row_block(2 * phase), 2), z_, 1 - k]
            send(slot, slot, sib_ss.at[phase, number], sib_rs.at[phase, number], me).wait_recv()
        else:
            for j in (2 * phase, 2 * phase + 1):
                slot = pg.at[row_block(j), z_, 1 - k]
                send(slot, slot, last_ss.at[j], last_rs.at[j], me).wait_recv()
        rows = pg[pl.ds(row_block(2 * phase), 2), z_].reshape(256, COLS)
        product = dot(rows, gc[...]).astype(BF16)
        for part in range(2):
            sx[phase, number, part] = product[128 * part : 128 * part + 128]
            remote, copy = x_copy(phase, number, part)

            @pl.when(remote)
            def _():
                copy.start()

    def x_sum(phase, number):
        zq = group_z(number) % 4
        total = sx[phase, number, x // 2].astype(F32)
        for index in range(NX - 1):
            slot = rx.at[phase, index, zq]
            send(slot, slot, xs_ss.at[phase, 0, 0], xs_rs.at[phase, index, zq], me).wait_recv()
            total = total + rx[phase, index, zq].astype(F32)
        return total

    def yh_copy(zq):
        return send(ysend.at[zq], yrecv.at[zq], yh_ss.at[zq], yh_rs.at[zq], other_half)

    def pass_half(number):
        @pl.when(group_z(number) // 4 == x % 2)
        def _():
            zq = group_z(number) % 4
            ysend[zq] = x_sum(0, number).astype(BF16)
            yh_copy(zq).start()

    def finish(number):
        @pl.when(group_z(number) // 4 == x % 2)
        def _():
            zq = group_z(number) % 4
            yh_copy(zq).wait_recv()
            value = x_sum(1, number) + yrecv[zq].astype(F32)
            out_ref[:, pl.ds(pl.multiple_of(zq * 128, 128), 128)] = value.T.astype(BF16)

    multiply(0, 0)

    lags[0] = dot(lag_ref[...], q_pos[...]).astype(BF16).reshape(2, NY, 32, COLS)
    negative = dot(q_neg[...], rev[...]).astype(BF16)
    lags[1] = dot(lag_ref[...], negative).astype(BF16).reshape(2, NY, 32, COLS)
    go(send(lags.at[:, 1 - k], kbuf, k_ss.at[0], k_rs.at[0], sibling))
    serve(0, 1)
    serve(1, 1)
    send(kbuf, kbuf, k_ss.at[0], k_rs.at[0], me).wait_recv()
    for i in range(2):
        for y_ in range(NY):
            half_sum[y_, i] = (lags[i, k, y_].astype(F32) + kbuf[i, y_].astype(F32)).astype(BF16)
    for d in range(1, NY):
        go(send(half_sum.at[(y + d) % NY], ybuf.at[d - 1], y_ss.at[d - 1], y_rs.at[d - 1], along_y(d)))
    serve_own(3)
    serve(0, 2)
    multiply(0, 1)
    multiply(0, 2)
    pass_half(0)
    serve(1, 2)
    serve(0, 3)
    multiply(0, 3)
    multiply(0, 4)
    pass_half(1)
    pass_half(2)
    serve(1, 3)
    multiply(1, 0)
    serve(0, 4)
    multiply(0, 5)
    multiply(0, 6)
    for d in range(1, NY):
        slot = ybuf.at[d - 1]
        send(slot, slot, y_ss.at[d - 1], y_rs.at[d - 1], me).wait_recv()
    for i in range(2):
        total = half_sum[y, i].astype(F32)
        for d in range(1, NY):
            total = total + ybuf[d - 1, i].astype(F32)
        for z_ in range(NZ):
            zsum[i, z_] = total[4 * z_ : 4 * z_ + 4]
    for d in range(NZ):
        to = (z + d) % NZ
        go(send(zsum.at[1, to], zneg.at[d], z_ss.at[1, d], z_rs.at[1, d], mirror(d)))
        if d > 0:
            go(send(zsum.at[0, to], zpos.at[d - 1], z_ss.at[0, d], z_rs.at[0, d], along_z(d)))
    multiply(1, 1)
    multiply(1, 2)
    pass_half(3)
    pass_half(4)
    serve(1, 4)
    multiply(0, 7)
    multiply(1, 3)
    multiply(1, 4)
    multiply(1, 5)
    multiply(1, 6)
    multiply(1, 7)
    pass_half(5)
    pass_half(6)
    pass_half(7)
    finish(0)
    finish(1)
    finish(2)
    finish(3)
    finish(4)
    finish(5)
    finish(6)
    total = zsum[0, z]
    for d in range(NZ):
        send(zneg.at[d], zneg.at[d], z_ss.at[1, d], z_rs.at[1, d], me).wait_recv()
        total = total + zneg[d]
        if d > 0:
            send(zpos.at[d - 1], zpos.at[d - 1], z_ss.at[0, d], z_rs.at[0, d], me).wait_recv()
            total = total + zpos[d - 1]
    fg_ref[...] = total * (1.0 / math.sqrt(16384))
    finish(7)

    @pl.when(serves)
    def _():
        for copy in served:
            copy.wait_send()

    for j in range(NY):
        for way in range(2):
            for step in (1, 2, 3, 4) if j % 2 == way else (1, 2, 3):
                hop(way, step, j).wait_send()
    for copy in pending:
        copy.wait_send()
    for zq in range(4):
        yh_copy(zq).wait_send()
    for phase in range(2):
        for number in range(8):
            for part in range(2):
                remote, copy = x_copy(phase, number, part)

                @pl.when(remote)
                def _():
                    copy.wait_send()


def body(grad_out, saved_in, filter_taps, skip_gain, projection):
    basis = half_bin_basis(ROWS)
    inverse = basis.T / ROWS

    def bf16(values):
        return jnp.asarray(values.astype(ml_dtypes.bfloat16))

    vmem, dma = pltpu.VMEM, pltpu.SemaphoreType.DMA
    square = vmem((2 * ROWS, COLS), F32)
    packed = vmem((2 * ROWS, COLS), BF16)
    block = vmem((ROWS, COLS), BF16)
    scratch = [
        block, block, block, vmem((1, COLS), F32), vmem((2 * ROWS, ROWS), BF16), block, block, dma((8,)),
        vmem((2, ROWS, COLS), BF16),
        vmem((4, 64, COLS), BF16),
        vmem((NY, NZ, 2, 64, COLS), BF16),
        vmem((2, NZ, 2, 128, ROWS), BF16),
        vmem((2, NX - 1, 4, 128, ROWS), BF16),
        vmem((4, 128, ROWS), BF16),
        vmem((4, 128, ROWS), BF16),
        vmem((COLS, ROWS), BF16),
        vmem((COLS, COLS), BF16),
        square, square, square, square, square, square, packed, packed, packed,
        vmem((2, 2, NY, 32, COLS), BF16),
        vmem((2, NY, 32, COLS), BF16),
        vmem((NY, 2, 32, COLS), BF16),
        vmem((NY - 1, 2, 32, COLS), BF16),
        vmem((2, NZ, 4, COLS), F32),
        vmem((NZ - 1, 4, COLS), F32),
        vmem((NZ, 4, COLS), F32),
        dma((2,)), dma((4,)), dma((4,)), dma((2,)), dma((2,)), dma((3,)), dma((4,)),
        dma((2, 4, 4)), dma((2, 4, 4)), dma((2, 7)), dma((2, 7)), dma((4,)), dma((4,)),
        dma((2, 8, 2)), dma((2, 3, 4)), dma((4,)), dma((4,)), dma((1,)), dma((1,)),
        dma((3,)), dma((3,)), dma((2, 8)), dma((2, 8)),
    ]
    return pl.pallas_call(
        kernel,
        out_shape=(jax.ShapeDtypeStruct((ROWS, COLS), BF16), jax.ShapeDtypeStruct((4, COLS), F32)),
        in_specs=[pl.BlockSpec(memory_space=pltpu.HBM)] * 8,
        out_specs=(pl.BlockSpec(memory_space=vmem), pl.BlockSpec(memory_space=vmem)),
        scratch_shapes=scratch,
        compiler_params=pltpu.CompilerParams(
            collective_id=0, has_side_effects=True, vmem_limit_bytes=63 << 20
        ),
        name="conv_backward",
    )(
        grad_out, saved_in, filter_taps, skip_gain.reshape(1, COLS), projection,
        bf16(basis), bf16(inverse), bf16(inverse[lag_order()]),
    )


def solution(mesh):
    placed = (P("seq", "ch"), P("seq", "ch"), P(None, "ch"), P("ch"), P("seq", "ch"))
    return jax.shard_map(
        body,
        mesh=mesh,
        in_specs=placed,
        out_specs=(P("seq", "ch"), P("seq", "ch")),
        check_vma=False,
    )
```

time: 85 us -> 73.2 us (0.86)
  the two profiles are of different devices: /device:TPU:71 before, /device:TPU:75 now
where the time goes in v3:
time: 73.2 us; the launch traced here: 73 us
  Pallas kernels  70.1 us (96%)
  local copies, waits for them, and re-layouts  2.28 us (3%)
    pallas_call x1, Pallas kernels, body(): pl.pallas_call(kernel, out_shape=(jax.ShapeDtypeStruct((ROWS, COLS), BF16...  70.1 us
    unnamed x4, local copies, waits for them, and re-layouts  2.28 us

profile of v3, /device:TPU:75, one launch (start us, length us, event | category | flops | bytes accessed | tf_op | source)
XLA Modules:
  0.0 73.0 jit_solution(14843619130609557314)
XLA Ops:
  0.6 70.1 %conv_backward.1 = (bf16[256,512]{1,0:T(8,128)(2,1)}, f32[4,512]{1,0:T(4,128)}) custom-call(bf16[256,512]{1,0:T(8,128)(2,1)} %g_hbm.1, bf16[256,512]{1,0:T(8,128)(2,1)} %x_hbm.1, bf16[256,512]{1,0:T(8,128)(2,1)} %f_hbm.1, f32[1,512]{1,0:T(1,128)} %bitcast.1, bf16[64,512]{1,0:T(8,128)(2,1)} %p_hbm.1, bf16[512,256]{1,0:T(8,128)(2,1)} %constant.6.clone.fwd_hbm, ...), custom_call_target="tpu_custom_call" | custom-call | tf_op jit(solution)/shard_map/conv_backward/pallas_call | solution.py:425
  70.8 0.0 copy-start
  70.8 1.7 %copy.12 = bf16[256,512]{1,0:T(8,128)(2,1)} copy(bf16[256,512]{1,0:T(8,128)(2,1)} %get-tuple-element.4) | data formatting | bytes 524288
  72.4 0.0 copy-done
  72.4 0.6 copy.13
Async XLA Ops:
  70.8 1.7 %copy-start = (f32[4,512]{1,0:T(4,128)S(1)}, f32[4,512]{1,0:T(4,128)}, u32[]{:S(2)}) copy-start(f32[4,512]{1,0:T(4,128)} %get-tuple-element.5) | copy-start | bytes 24580

commit v4 on v3

--- a/solution.py
+++ b/solution.py
@@ -290,35 +290,46 @@
             out_ref[:, pl.ds(pl.multiple_of(zq * 128, 128), 128)] = value.T.astype(BF16)
 
     multiply(0, 0)
+    multiply(1, 0)
+    serve(0, 1)
+    serve(1, 1)
 
     lags[0] = dot(lag_ref[...], q_pos[...]).astype(BF16).reshape(2, NY, 32, COLS)
     negative = dot(q_neg[...], rev[...]).astype(BF16)
     lags[1] = dot(lag_ref[...], negative).astype(BF16).reshape(2, NY, 32, COLS)
     go(send(lags.at[:, 1 - k], kbuf, k_ss.at[0], k_rs.at[0], sibling))
-    serve(0, 1)
-    serve(1, 1)
+    serve_own(3)
+    multiply(0, 1)
+    multiply(0, 2)
+    serve(0, 2)
     send(kbuf, kbuf, k_ss.at[0], k_rs.at[0], me).wait_recv()
     for i in range(2):
         for y_ in range(NY):
             half_sum[y_, i] = (lags[i, k, y_].astype(F32) + kbuf[i, y_].astype(F32)).astype(BF16)
     for d in range(1, NY):
         go(send(half_sum.at[(y + d) % NY], ybuf.at[d - 1], y_ss.at[d - 1], y_rs.at[d - 1], along_y(d)))
-    serve_own(3)
-    serve(0, 2)
-    multiply(0, 1)
-    multiply(0, 2)
-    pass_half(0)
     serve(1, 2)
-    serve(0, 3)
     multiply(0, 3)
     multiply(0, 4)
+    pass_half(0)
+    serve(0, 3)
+    serve(1, 3)
     pass_half(1)
     pass_half(2)
-    serve(1, 3)
-    multiply(1, 0)
-    serve(0, 4)
     multiply(0, 5)
     multiply(0, 6)
+    serve(0, 4)
+    serve(1, 4)
+    multiply(0, 7)
+    multiply(1, 1)
+    multiply(1, 2)
+    multiply(1, 3)
+    multiply(1, 4)
+    multiply(1, 5)
+    multiply(1, 6)
+    multiply(1, 7)
+    pass_half(3)
+    pass_half(4)
     for d in range(1, NY):
         slot = ybuf.at[d - 1]
         send(slot, slot, y_ss.at[d - 1], y_rs.at[d - 1], me).wait_recv()
@@ -333,17 +344,6 @@
         go(send(zsum.at[1, to], zneg.at[d], z_ss.at[1, d], z_rs.at[1, d], mirror(d)))
         if d > 0:
             go(send(zsum.at[0, to], zpos.at[d - 1], z_ss.at[0, d], z_rs.at[0, d], along_z(d)))
-    multiply(1, 1)
-    multiply(1, 2)
-    pass_half(3)
-    pass_half(4)
-    serve(1, 4)
-    multiply(0, 7)
-    multiply(1, 3)
-    multiply(1, 4)
-    multiply(1, 5)
-    multiply(1, 6)
-    multiply(1, 7)
     pass_half(5)
     pass_half(6)
     pass_half(7)

time: 73.2 us -> 71.4 us (0.975)
  the two profiles are of different devices: /device:TPU:75 before, /device:TPU:71 now
where the time goes in v4:
time: 71.4 us; the launch traced here: 71.2 us
  Pallas kernels  68.3 us (96%)
  local copies, waits for them, and re-layouts  2.28 us (3%)
    pallas_call x1, Pallas kernels, body(): pl.pallas_call(kernel, out_shape=(jax.ShapeDtypeStruct((ROWS, COLS), BF16...  68.3 us
    unnamed x4, local copies, waits for them, and re-layouts  2.28 us

profile of v4, /device:TPU:71, one launch (start us, length us, event | category | flops | bytes accessed | tf_op | source)
XLA Modules:
  0.0 71.2 jit_solution(12846993322545400153)
XLA Ops:
  0.6 68.3 %conv_backward.1 = (bf16[256,512]{1,0:T(8,128)(2,1)}, f32[4,512]{1,0:T(4,128)}) custom-call(bf16[256,512]{1,0:T(8,128)(2,1)} %g_hbm.1, bf16[256,512]{1,0:T(8,128)(2,1)} %x_hbm.1, bf16[256,512]{1,0:T(8,128)(2,1)} %f_hbm.1, f32[1,512]{1,0:T(1,128)} %bitcast.1, bf16[64,512]{1,0:T(8,128)(2,1)} %p_hbm.1, bf16[512,256]{1,0:T(8,128)(2,1)} %constant.6.clone.fwd_hbm, ...), custom_call_target="tpu_custom_call" | custom-call | tf_op jit(solution)/shard_map/conv_backward/pallas_call | solution.py:425
  68.9 0.0 copy-start
  69.0 1.7 %copy.12 = bf16[256,512]{1,0:T(8,128)(2,1)} copy(bf16[256,512]{1,0:T(8,128)(2,1)} %get-tuple-element.4) | data formatting | bytes 524288
  70.6 0.0 copy-done
  70.6 0.6 copy.13
Async XLA Ops:
  68.9 1.7 %copy-start = (f32[4,512]{1,0:T(4,128)S(1)}, f32[4,512]{1,0:T(4,128)}, u32[]{:S(2)}) copy-start(f32[4,512]{1,0:T(4,128)} %get-tuple-element.5) | copy-start | bytes 24580

commit v5 on v4

--- a/solution.py
+++ b/solution.py
@@ -328,8 +328,6 @@
     multiply(1, 5)
     multiply(1, 6)
     multiply(1, 7)
-    pass_half(3)
-    pass_half(4)
     for d in range(1, NY):
         slot = ybuf.at[d - 1]
         send(slot, slot, y_ss.at[d - 1], y_rs.at[d - 1], me).wait_recv()
@@ -344,6 +342,8 @@
         go(send(zsum.at[1, to], zneg.at[d], z_ss.at[1, d], z_rs.at[1, d], mirror(d)))
         if d > 0:
             go(send(zsum.at[0, to], zpos.at[d - 1], z_ss.at[0, d], z_rs.at[0, d], along_z(d)))
+    pass_half(3)
+    pass_half(4)
     pass_half(5)
     pass_half(6)
     pass_half(7)

time: 71.4 us -> 71.4 us (level)
  no operation moved by 1% of the time
where the time goes in v5:
time: 71.4 us; the launch traced here: 71.2 us
  Pallas kernels  68.3 us (96%)
  local copies, waits for them, and re-layouts  2.28 us (3%)
    pallas_call x1, Pallas kernels, body(): pl.pallas_call(kernel, out_shape=(jax.ShapeDtypeStruct((ROWS, COLS), BF16...  68.3 us
    unnamed x4, local copies, waits for them, and re-layouts  2.28 us

profile of v5, /device:TPU:71, one launch (start us, length us, event | category | flops | bytes accessed | tf_op | source)
XLA Modules:
  0.0 71.2 jit_solution(8877542072451660604)
XLA Ops:
  0.6 68.3 %conv_backward.1 = (bf16[256,512]{1,0:T(8,128)(2,1)}, f32[4,512]{1,0:T(4,128)}) custom-call(bf16[256,512]{1,0:T(8,128)(2,1)} %g_hbm.1, bf16[256,512]{1,0:T(8,128)(2,1)} %x_hbm.1, bf16[256,512]{1,0:T(8,128)(2,1)} %f_hbm.1, f32[1,512]{1,0:T(1,128)} %bitcast.1, bf16[64,512]{1,0:T(8,128)(2,1)} %p_hbm.1, bf16[512,256]{1,0:T(8,128)(2,1)} %constant.6.clone.fwd_hbm, ...), custom_call_target="tpu_custom_call" | custom-call | tf_op jit(solution)/shard_map/conv_backward/pallas_call | solution.py:425
  68.9 0.0 copy-start
  69.0 1.7 %copy.12 = bf16[256,512]{1,0:T(8,128)(2,1)} copy(bf16[256,512]{1,0:T(8,128)(2,1)} %get-tuple-element.4) | data formatting | bytes 524288
  70.6 0.0 copy-done
  70.6 0.6 copy.13
Async XLA Ops:
  68.9 1.7 %copy-start = (f32[4,512]{1,0:T(4,128)S(1)}, f32[4,512]{1,0:T(4,128)}, u32[]{:S(2)}) copy-start(f32[4,512]{1,0:T(4,128)} %get-tuple-element.5) | copy-start | bytes 24580
